TPU v7x, 32 devices: a whole 2x2x4 slice. The times are simulated.
32 devices in a mesh: freq: 4 (over y, core), tile: 8 (over z, x).
Axes of the slice: x: 2, y: 2, z: 4, core: 2. Of those that a mesh axis runs over, the one named last changes fastest.
Arguments:
- wavefield: bfloat16 [4, 3072, 256], P('freq', 'tile'), may hold values from -6 to 6
- column_bases: bfloat16 [4, 8, 8, 384, 256], P('freq', 'tile'), may hold values from -0.3125 to 0.3125
- row_bases: bfloat16 [4, 8, 8, 384, 256], P('freq', 'tile'), may hold values from -0.1875 to 0.1875
- tile_ranks: int32 [8, 8], replicated, may hold values from 16 to 128, as said below
- row_order: int32 [8], replicated, may hold values from 0 to 7, each once
- shrink_level: float32 [128], P('freq'), may hold values from 0.5 to 3
Outputs:
- shrunk: float32 [12, 128, 3072], P(None, 'freq', 'tile')
Inputs may be any that keep to these rules, and one draw needn't show every extreme that they name: `tile_ranks`: each tile's rank lies between 16 and 128; both ends occur in every draw. `row_order`: A permutation of the 8 tile rows.
All inputs are finite; a program needn't handle non-finite values.
Results may differ from a plain program's by a relative error of at most 0.0044.
Values may be sent and summed in bfloat16 or wider, within the bound.
A program may use at most 64 MiB of HBM per device.

v0:
```python
import functools
import math

import jax
import jax.numpy as jnp
from jax import lax
from jax.experimental import pallas as pl
from jax.experimental.pallas import tpu as pltpu
from jax.sharding import PartitionSpec as P

MESH = pl.DeviceIdType.MESH


def partner(me, m, n):
    other = me
    bit = 1
    while bit < n:
        if m & bit:
            other = other + bit * (1 - 2 * (lax.div(me, bit) % 2))
        bit *= 2
    return other


def exchange_kernel(n, nf, wave, v_hbm, u_hbm, table_hbm,
                    spec_out,
                    x_buf, v_buf, u_buf, table, sending, landing,
                    spec_sending, spec_landing,
                    load_sems, v_sems, send_sems, recv_sems, spec_send_sems, spec_recv_sems):
    tile = lax.axis_index("tile")
    freq = lax.axis_index("freq")
    tile_rows = x_buf.shape[0]
    sources = x_buf.shape[1] // 2
    width = v_buf.shape[2] // 2
    chunk = sources // nf
    far = sorted(range(n // 2, n), key=lambda m: (m // 2, -m))
    near = list(range(n // 2 - 1, 0, -1))
    steps = far + near
    arrivals = near + far

    x_load = pltpu.make_async_copy(wave.at[0], x_buf, load_sems.at[0])
    v_loads = [pltpu.make_async_copy(v_hbm.at[0, 0, i], v_buf.at[i], v_sems.at[i]) for i in range(n)]
    small_loads = [pltpu.make_async_copy(table_hbm, table, load_sems.at[2])]
    u_load = pltpu.make_async_copy(u_hbm.at[0, 0], u_buf, load_sems.at[1])

    barrier = pltpu.get_barrier_semaphore()
    for m in steps:
        pl.semaphore_signal(
            barrier, inc=1, device_id={"tile": partner(tile, m, n)}, device_id_type=MESH
        )
    for hop in range(1, nf):
        pl.semaphore_signal(
            barrier, inc=1, device_id={"freq": (freq + hop) % nf}, device_id_type=MESH
        )

    x_load.start()
    for load in small_loads + v_loads:
        load.start()

    def chunk_of(p):
        return (freq + 1 + p) % nf

    def send(p, m):
        return pltpu.make_async_remote_copy(
            src_ref=sending.at[m, chunk_of(p)],
            dst_ref=landing.at[p, m],
            send_sem=send_sems.at[p, m],
            recv_sem=recv_sems.at[p, m],
            device_id={"tile": partner(tile, m, n)},
            device_id_type=MESH,
        )

    def spec_send(p):
        return pltpu.make_async_remote_copy(
            src_ref=spec_sending.at[p],
            dst_ref=spec_landing.at[freq],
            send_sem=spec_send_sems.at[p],
            recv_sem=spec_recv_sems.at[p],
            device_id={"freq": chunk_of(p)},
            device_id_type=MESH,
        )

    x_load.wait()
    x_t = x_buf[...].T
    for load in small_loads + v_loads:
        load.wait()
    u_load.start()

    lane = lax.broadcasted_iota(jnp.int32, (sources, width), 1)

    def make_block(m):
        row = table[n, partner(tile, m, n)]
        rank = table[row, tile]
        product = jnp.dot(x_t, v_buf[row], preferred_element_type=jnp.float32)
        keep = lane < rank
        real = product[:sources, :width] + product[sources:, width:]
        imag = product[sources:, :width] - product[:sources, width:]
        real = jnp.where(keep, real, 0.0).astype(jnp.bfloat16)
        imag = jnp.where(keep, imag, 0.0).astype(jnp.bfloat16)
        for c in range(nf):
            sending[m, c, 0] = real[c * chunk:(c + 1) * chunk]
            sending[m, c, 1] = imag[c * chunk:(c + 1) * chunk]

    make_block(steps[0])
    pl.semaphore_wait(barrier, n - 1 + nf - 1)
    for index, m in enumerate(steps):
        make_block(steps[index + 1] if index + 1 < len(steps) else 0)
        send(0, m).start()
    for p in range(1, nf):
        for m in steps:
            send(p, m).start()

    u_load.wait()

    def apply_rows(pair, source):
        real, imag = pair[0], pair[1]
        left = jnp.concatenate(
            [jnp.concatenate([real, -imag], axis=1), jnp.concatenate([imag, real], axis=1)], axis=0
        )
        return lax.dot_general(
            left, u_buf[source], (((1,), (1,)), ((), ())), preferred_element_type=jnp.float32
        )

    for p in range(nf):
        total = apply_rows(sending[0, chunk_of(p)], tile)
        for m in arrivals:
            send(p, m).wait_recv()
            total = total + apply_rows(landing[p, m], partner(tile, m, n))
        spectrum = total.astype(jnp.bfloat16).reshape(2, chunk, tile_rows)
        if p < nf - 1:
            spec_sending[p] = spectrum
            spec_send(p).start()
        else:
            spec_out[freq] = spectrum

    for p in range(nf - 1):
        spec_send(p).wait_recv()
        source = (freq + nf - 1 - p) % nf
        spec_out[source] = spec_landing[source]
    for p in range(nf):
        for m in steps:
            send(p, m).wait_send()
    for p in range(nf - 1):
        spec_send(p).wait_send()


def shrink_kernel(nf, nt, spec, level, out, held, sems):
    rows, tile_rows = spec.shape[2], spec.shape[3]
    half = nt // 2
    scale = 1.0 / math.sqrt(nf)
    band = 16 if rows % 16 == 0 else rows
    lanes = 128

    def coefficient(func, f, t):
        value = func(2.0 * math.pi * ((f + 1) * t % nt) / nt)
        return 0.0 if abs(value) < 1e-12 else value * scale

    lane_v = lax.broadcasted_iota(jnp.int32, (rows, rows), 1)
    row_v = lax.broadcasted_iota(jnp.int32, (rows, rows), 0)
    square = jnp.broadcast_to(level[...] * level[...], (rows, rows))
    column = jnp.sum(jnp.where(lane_v == row_v, square, 0.0), axis=1, keepdims=True)
    squares = jnp.broadcast_to(column, (rows, lanes))
    copies = []
    for r in range(0, rows, band):
        lvl = squares[r:r + band, :]
        for l in range(0, tile_rows, lanes):
            values = [
                [spec[f, c, r:r + band, l:l + lanes].astype(jnp.float32) for c in range(2)]
                for f in range(nf)
            ]
            for t in range(half):
                sums = [None, None]
                for f in range(nf):
                    kind = (f + 1) % 2
                    terms = (
                        (coefficient(math.cos, f, t), values[f][0]),
                        (-coefficient(math.sin, f, t), values[f][1]),
                    )
                    for factor, value in terms:
                        if factor == 0.0:
                            continue
                        term = value * factor
                        sums[kind] = term if sums[kind] is None else sums[kind] + term
                even, odd = sums
                for place, signal in ((t, even + odd), (t + half, even - odd)):
                    power = signal * signal
                    held[place, r:r + band, l:l + lanes] = power * signal / (power + lvl)
        copy = pltpu.make_async_copy(
            held.at[:, pl.ds(r, band)], out.at[:, pl.ds(r, band)], sems.at[r // band]
        )
        copy.start()
        copies.append(copy)
    for copy in copies:
        copy.wait()


def body(n, nf, wavefield, column_bases, row_bases, tile_ranks, row_order, shrink_level):
    _, tile_rows, double_sources = wavefield.shape
    sources = double_sources // 2
    double_width = column_bases.shape[4]
    width = double_width // 2
    chunk = sources // nf
    nt = 3 * nf
    hbm = pl.BlockSpec(memory_space=pltpu.HBM)
    vmem = pl.BlockSpec(memory_space=pltpu.VMEM)
    bf16 = jnp.bfloat16
    table = jnp.concatenate([tile_ranks, row_order[None]])
    spec = pl.pallas_call(
        functools.partial(exchange_kernel, n, nf),
        out_shape=jax.ShapeDtypeStruct((nf, 2, chunk, tile_rows), bf16),
        in_specs=[hbm] * 4,
        out_specs=vmem,
        scratch_shapes=[
            pltpu.VMEM((tile_rows, double_sources), bf16),
            pltpu.VMEM((n, tile_rows, double_width), bf16),
            pltpu.VMEM((n, tile_rows, double_width), bf16),
            pltpu.SMEM(table.shape, jnp.int32),
            pltpu.VMEM((n, nf, 2, chunk, width), bf16),
            pltpu.VMEM((nf, n, 2, chunk, width), bf16),
            pltpu.VMEM((nf - 1, 2, chunk, tile_rows), bf16),
            pltpu.VMEM((nf, 2, chunk, tile_rows), bf16),
            pltpu.SemaphoreType.DMA((3,)),
            pltpu.SemaphoreType.DMA((n,)),
            pltpu.SemaphoreType.DMA((nf, n)),
            pltpu.SemaphoreType.DMA((nf, n)),
            pltpu.SemaphoreType.DMA((nf - 1,)),
            pltpu.SemaphoreType.DMA((nf - 1,)),
        ],
        compiler_params=pltpu.CompilerParams(
            collective_id=0, has_side_effects=True, vmem_limit_bytes=56_250_000
        ),
        name="exchange",
    )(wavefield, column_bases, row_bases, table)
    return pl.pallas_call(
        functools.partial(shrink_kernel, nf, nt),
        out_shape=jax.ShapeDtypeStruct((nt, chunk, tile_rows), jnp.float32),
        in_specs=[vmem, vmem],
        out_specs=hbm,
        scratch_shapes=[
            pltpu.VMEM((nt, chunk, tile_rows), jnp.float32),
            pltpu.SemaphoreType.DMA((max(1, chunk // 16),)),
        ],
        compiler_params=pltpu.CompilerParams(vmem_limit_bytes=16 * 1024 * 1024),
        name="shrink",
    )(spec, shrink_level[None])


def solution(mesh):
    in_specs = (
        P("freq", "tile", None),
        P("freq", "tile", None, None, None),
        P("freq", "tile", None, None, None),
        P(),
        P(),
        P("freq"),
    )
    out_specs = P(None, "freq", "tile")
    return jax.shard_map(
        functools.partial(body, mesh.shape["tile"], mesh.shape["freq"]),
        mesh=mesh, in_specs=in_specs, out_specs=out_specs, check_vma=False,
    )
```

profile of v0, /device:TPU:1, one launch (start us, length us, event | category | flops | bytes accessed | tf_op | source)
XLA Modules:
  0.0 23.4 jit_solution(3550764058937877717)
XLA Ops:
  0.0 0.7 %pad_add_fusion.table_hbm = s32[9,8]{1,0:T(8,128)S(1)} fusion(s32[1,8]{1,0:T(1,128)} %bitcast.3, s32[8,8]{1,0:T(8,128)} %param.9), kind=kLoop, calls=%fused_computation | loop fusion | flops 72 | bytes 576 | tf_op jit(solution)/shard_map/concatenate | solution.py:206
  0.7 0.0 copy-start
  0.7 21.7 %exchange.1.spec = bf16[4,2,32,384]{3,2,1,0:T(8,128)(2,1)S(1)} custom-call(bf16[1,384,256]{2,1,0:T(8,128)(2,1)} %wave.1, bf16[1,1,8,384,256]{4,3,2,1,0:T(8,128)(2,1)} %v_hbm.1, bf16[1,1,8,384,256]{4,3,2,1,0:T(8,128)(2,1)} %u_hbm.1, s32[9,8]{1,0:T(8,128)S(1)} %pad_add_fusion.table_hbm), custom_call_target="tpu_custom_call" | custom-call | tf_op jit(solution)/shard_map/exchange/pallas_call | solution.py:207
  22.4 0.0 copy-done
  22.4 1.0 %shrink.1 = f32[12,32,384]{2,1,0:T(8,128)} custom-call(bf16[4,2,32,384]{3,2,1,0:T(8,128)(2,1)S(1)} %exchange.1.spec, f32[1,32]{1,0:T(1,128)S(1)} %bitcast.2), custom_call_target="tpu_custom_call" | custom-call | tf_op jit(solution)/shard_map/shrink/pallas_call | solution.py:233
Async XLA Ops:
  0.7 21.7 %copy-start = (f32[32]{0:T(128)S(1)}, f32[32]{0:T(128)}, u32[]{:S(2)}) copy-start(f32[32]{0:T(128)} %param.11) | copy-start | bytes 388
where the time goes:
time: 23.6 us; the launch traced here: 23.4 us
  Pallas kernels  22.6 us (96%)
  other arithmetic  0.71 us (3%)
    pallas_call x1, Pallas kernels, body(): pl.pallas_call(functools.partial(exchange_kernel, n, nf), out_shape=jax.S...  21.7 us
    pallas_call x1, Pallas kernels, body(): pl.pallas_call(functools.partial(shrink_kernel, nf, nt), out_shape=jax.Sh...  0.96 us
    concatenate x1, other arithmetic, body(): table = jnp.concatenate([tile_ranks, row_order[None]])  0.71 us

commit v1 on v0

v1 whole, which is shorter than its diff:
```python
import functools
import math

import jax
import jax.numpy as jnp
from jax import lax
from jax.experimental import pallas as pl
from jax.experimental.pallas import tpu as pltpu
from jax.sharding import PartitionSpec as P

MESH = pl.DeviceIdType.MESH


def target(tile, k, n):
    half = n // 2
    late = tile // half
    place = tile * late + (n - 1 - tile) * (1 - late)
    end = place // (n - n // 4)
    turn = (k + half * end) % (n - 1)
    other = turn + (turn + n - place) // n
    return other * late + (n - 1 - other) * (1 - late)


def exchange_kernel(n, nf, gs, wave, v_hbm, u_hbm, ranks_hbm, order_hbm,
                    spec_out,
                    x_buf, v_buf, u_buf, ranks, order, sending, landing,
                    spec_sending, spec_landing,
                    load_sems, v_sems, send_sems, recv_sems, spec_send_sems, spec_recv_sems):
    tile = lax.axis_index("tile")
    freq = lax.axis_index("freq")
    tile_rows = x_buf.shape[0]
    sources = x_buf.shape[1] // 2
    width = v_buf.shape[2] // 2
    chunk = sources // nf
    ng = nf // gs
    rows = gs * chunk
    targets = [target(tile, k, n) for k in range(n - 1)]

    loads = [
        pltpu.make_async_copy(wave.at[0], x_buf, load_sems.at[0]),
        pltpu.make_async_copy(ranks_hbm, ranks, load_sems.at[2]),
        pltpu.make_async_copy(order_hbm, order, load_sems.at[3]),
    ]
    v_loads = [pltpu.make_async_copy(v_hbm.at[0, 0, i], v_buf.at[i], v_sems.at[i]) for i in range(n)]
    u_load = pltpu.make_async_copy(u_hbm.at[0, 0], u_buf, load_sems.at[1])
    for load in loads + v_loads:
        load.start()

    barrier = pltpu.get_barrier_semaphore()
    for other in targets:
        pl.semaphore_signal(barrier, inc=1, device_id={"tile": other}, device_id_type=MESH)
    for hop in range(1, nf):
        pl.semaphore_signal(
            barrier, inc=1, device_id={"freq": (freq + hop) % nf}, device_id_type=MESH
        )

    def group_of(p):
        return (freq // gs + 1 + p) % ng

    def send(p, k):
        return pltpu.make_async_remote_copy(
            src_ref=sending.at[k, group_of(p)],
            dst_ref=landing.at[p, tile],
            send_sem=send_sems.at[p, k],
            recv_sem=recv_sems.at[p, tile],
            device_id={"tile": targets[k]},
            device_id_type=MESH,
        )

    def arrival(p, k):
        return pltpu.make_async_remote_copy(
            src_ref=sending.at[k, group_of(p)],
            dst_ref=landing.at[p, targets[k]],
            send_sem=send_sems.at[p, k],
            recv_sem=recv_sems.at[p, targets[k]],
            device_id={"tile": targets[k]},
            device_id_type=MESH,
        )

    def receiver_of(q):
        p, c = q // gs, q % gs
        return group_of(p) * gs + (freq + 1 + c) % gs

    def spec_send(q):
        return pltpu.make_async_remote_copy(
            src_ref=spec_sending.at[q],
            dst_ref=spec_landing.at[freq],
            send_sem=spec_send_sems.at[q],
            recv_sem=spec_recv_sems.at[freq],
            device_id={"freq": receiver_of(q)},
            device_id_type=MESH,
        )

    def spec_arrival(q, source):
        return pltpu.make_async_remote_copy(
            src_ref=spec_sending.at[q],
            dst_ref=spec_landing.at[source],
            send_sem=spec_send_sems.at[q],
            recv_sem=spec_recv_sems.at[source],
            device_id={"freq": receiver_of(q)},
            device_id_type=MESH,
        )

    for load in loads:
        load.wait()
    x_t = x_buf[...].T
    for load in v_loads:
        load.wait()
    u_load.start()

    lane = lax.broadcasted_iota(jnp.int32, (sources, width), 1)

    def make_block(k, slot):
        row = order[slot]
        rank = ranks[row, tile]
        product = jnp.dot(x_t, v_buf[row], preferred_element_type=jnp.float32)
        keep = lane < rank
        real = product[:sources, :width] + product[sources:, width:]
        imag = product[sources:, :width] - product[:sources, width:]
        real = jnp.where(keep, real, 0.0).astype(jnp.bfloat16)
        imag = jnp.where(keep, imag, 0.0).astype(jnp.bfloat16)
        for g in range(ng):
            sending[k, g, 0] = real[g * rows:(g + 1) * rows]
            sending[k, g, 1] = imag[g * rows:(g + 1) * rows]

    pairs = [list(range(k, min(k + 2, n - 1))) for k in range(0, n - 1, 2)]
    for index, pair in enumerate(pairs):
        for k in pair:
            make_block(k, targets[k])
        if index == 0:
            pl.semaphore_wait(barrier, n - 1 + nf - 1)
        for p in range(ng):
            for k in pair:
                send(p, k).start()
    make_block(n - 1, tile)

    u_load.wait()

    def apply_rows(pair, source):
        real, imag = pair[0], pair[1]
        left = jnp.concatenate(
            [jnp.concatenate([real, -imag], axis=1), jnp.concatenate([imag, real], axis=1)], axis=0
        )
        return lax.dot_general(
            left, u_buf[source], (((1,), (1,)), ((), ())), preferred_element_type=jnp.float32
        )

    half = n // 2
    arrivals = list(range(half, n - 1)) + list(range(half))
    for p in range(ng):
        total = apply_rows(sending[n - 1, group_of(p)], tile)
        for k in arrivals:
            arrival(p, k).wait_recv()
            total = total + apply_rows(landing[p, targets[k]], targets[k])
        spectrum = total.astype(jnp.bfloat16).reshape(2, gs, chunk, tile_rows)
        for c in range(gs):
            q = p * gs + c
            place = (freq + 1 + c) % gs
            part = spectrum[:, 0]
            for other in range(1, gs):
                part = jnp.where(place == other, spectrum[:, other], part)
            if q < nf - 1:
                spec_sending[q] = part
                spec_send(q).start()
            else:
                spec_out[freq] = part

    for q in range(nf - 1):
        p, c = q // gs, q % gs
        source = ((freq // gs + ng - 1 - p) % ng) * gs + (freq + 1 + c) % gs
        spec_arrival(q, source).wait_recv()
        spec_out[source] = spec_landing[source]
    for p in range(ng):
        for k in range(n - 1):
            send(p, k).wait_send()
    for q in range(nf - 1):
        spec_send(q).wait_send()


def shrink_kernel(nf, nt, spec, level, out, held, sems):
    rows, tile_rows = spec.shape[2], spec.shape[3]
    half = nt // 2
    scale = 1.0 / math.sqrt(nf)
    band = 16 if rows % 16 == 0 else rows
    lanes = 128

    def coefficient(func, f, t):
        value = func(2.0 * math.pi * ((f + 1) * t % nt) / nt)
        return 0.0 if abs(value) < 1e-12 else value * scale

    lane_v = lax.broadcasted_iota(jnp.int32, (rows, rows), 1)
    row_v = lax.broadcasted_iota(jnp.int32, (rows, rows), 0)
    square = jnp.broadcast_to(level[...] * level[...], (rows, rows))
    column = jnp.sum(jnp.where(lane_v == row_v, square, 0.0), axis=1, keepdims=True)
    squares = jnp.broadcast_to(column, (rows, lanes))
    copies = []
    for r in range(0, rows, band):
        lvl = squares[r:r + band, :]
        for l in range(0, tile_rows, lanes):
            values = [
                [spec[f, c, r:r + band, l:l + lanes].astype(jnp.float32) for c in range(2)]
                for f in range(nf)
            ]
            for t in range(half):
                sums = [None, None]
                for f in range(nf):
                    kind = (f + 1) % 2
                    terms = (
                        (coefficient(math.cos, f, t), values[f][0]),
                        (-coefficient(math.sin, f, t), values[f][1]),
                    )
                    for factor, value in terms:
                        if factor == 0.0:
                            continue
                        term = value * factor
                        sums[kind] = term if sums[kind] is None else sums[kind] + term
                even, odd = sums
                for place, signal in ((t, even + odd), (t + half, even - odd)):
                    power = signal * signal
                    held[place, r:r + band, l:l + lanes] = power * signal / (power + lvl)
        copy = pltpu.make_async_copy(
            held.at[:, pl.ds(r, band)], out.at[:, pl.ds(r, band)], sems.at[r // band]
        )
        copy.start()
        copies.append(copy)
    for copy in copies:
        copy.wait()


def body(n, nf, wavefield, column_bases, row_bases, tile_ranks, row_order, shrink_level):
    _, tile_rows, double_sources = wavefield.shape
    sources = double_sources // 2
    double_width = column_bases.shape[4]
    width = double_width // 2
    chunk = sources // nf
    nt = 3 * nf
    gs = 2 if nf % 2 == 0 else 1
    ng = nf // gs
    hbm = pl.BlockSpec(memory_space=pltpu.HBM)
    vmem = pl.BlockSpec(memory_space=pltpu.VMEM)
    bf16 = jnp.bfloat16
    tables = [pltpu.with_memory_space_constraint(a, pltpu.HBM) for a in (tile_ranks, row_order)]
    spec = pl.pallas_call(
        functools.partial(exchange_kernel, n, nf, gs),
        out_shape=jax.ShapeDtypeStruct((nf, 2, chunk, tile_rows), bf16),
        in_specs=[hbm] * 5,
        out_specs=vmem,
        scratch_shapes=[
            pltpu.VMEM((tile_rows, double_sources), bf16),
            pltpu.VMEM((n, tile_rows, double_width), bf16),
            pltpu.VMEM((n, tile_rows, double_width), bf16),
            pltpu.SMEM(tile_ranks.shape, jnp.int32),
            pltpu.SMEM(row_order.shape, jnp.int32),
            pltpu.VMEM((n, ng, 2, gs * chunk, width), bf16),
            pltpu.VMEM((ng, n, 2, gs * chunk, width), bf16),
            pltpu.VMEM((nf - 1, 2, chunk, tile_rows), bf16),
            pltpu.VMEM((nf, 2, chunk, tile_rows), bf16),
            pltpu.SemaphoreType.DMA((4,)),
            pltpu.SemaphoreType.DMA((n,)),
            pltpu.SemaphoreType.DMA((ng, n)),
            pltpu.SemaphoreType.DMA((ng, n)),
            pltpu.SemaphoreType.DMA((nf,)),
            pltpu.SemaphoreType.DMA((nf,)),
        ],
        compiler_params=pltpu.CompilerParams(
            collective_id=0, has_side_effects=True, vmem_limit_bytes=56_250_000
        ),
        name="exchange",
    )(wavefield, column_bases, row_bases, *tables)
    return pl.pallas_call(
        functools.partial(shrink_kernel, nf, nt),
        out_shape=jax.ShapeDtypeStruct((nt, chunk, tile_rows), jnp.float32),
        in_specs=[vmem, vmem],
        out_specs=hbm,
        scratch_shapes=[
            pltpu.VMEM((nt, chunk, tile_rows), jnp.float32),
            pltpu.SemaphoreType.DMA((max(1, chunk // 16),)),
        ],
        compiler_params=pltpu.CompilerParams(vmem_limit_bytes=16 * 1024 * 1024),
        name="shrink",
    )(spec, shrink_level[None])


def solution(mesh):
    in_specs = (
        P("freq", "tile", None),
        P("freq", "tile", None, None, None),
        P("freq", "tile", None, None, None),
        P(),
        P(),
        P("freq"),
    )
    out_specs = P(None, "freq", "tile")
    return jax.shard_map(
        functools.partial(body, mesh.shape["tile"], mesh.shape["freq"]),
        mesh=mesh, in_specs=in_specs, out_specs=out_specs, check_vma=False,
    )
```

time: 23.6 us -> 21.6 us (0.915)
  the two profiles are of different devices: /device:TPU:1 before, /device:TPU:0 now
where the time goes in v1:
time: 21.6 us; the launch traced here: 21.5 us
  Pallas kernels  21.5 us (100%)
    pallas_call x1, Pallas kernels, body(): pl.pallas_call(functools.partial(exchange_kernel, n, nf, gs), out_shape=j...  20.5 us
    pallas_call x1, Pallas kernels, body(): pl.pallas_call(functools.partial(shrink_kernel, nf, nt), out_shape=jax.Sh...  0.96 us

profile of v1, /device:TPU:0, one launch (start us, length us, event | category | flops | bytes accessed | tf_op | source)
XLA Modules:
  0.0 21.5 jit_solution(1991543014756790289)
XLA Ops:
  0.0 0.0 copy-start
  0.0 20.5 %exchange.1.spec = bf16[4,2,32,384]{3,2,1,0:T(8,128)(2,1)S(1)} custom-call(bf16[1,384,256]{2,1,0:T(8,128)(2,1)} %wave.1, bf16[1,1,8,384,256]{4,3,2,1,0:T(8,128)(2,1)} %v_hbm.1, bf16[1,1,8,384,256]{4,3,2,1,0:T(8,128)(2,1)} %u_hbm.1, s32[8,8]{1,0:T(8,128)} %ranks_hbm.1, s32[8]{0:T(128)} %order_hbm.1), custom_call_target="tpu_custom_call" | custom-call | tf_op jit(solution)/shard_map/exchange/pallas_call | solution.py:243
  20.5 0.0 copy-done
  20.5 1.0 %shrink.1 = f32[12,32,384]{2,1,0:T(8,128)} custom-call(bf16[4,2,32,384]{3,2,1,0:T(8,128)(2,1)S(1)} %exchange.1.spec, f32[1,32]{1,0:T(1,128)S(1)} %bitcast.1), custom_call_target="tpu_custom_call" | custom-call | tf_op jit(solution)/shard_map/shrink/pallas_call | solution.py:270
Async XLA Ops:
  0.0 20.5 %copy-start = (f32[32]{0:T(128)S(1)}, f32[32]{0:T(128)}, u32[]{:S(2)}) copy-start(f32[32]{0:T(128)} %param.11) | copy-start | bytes 388

commit v2 on v1

--- a/solution.py
+++ b/solution.py
@@ -14,11 +14,13 @@
 def target(tile, k, n):
     half = n // 2
     late = tile // half
-    place = tile * late + (n - 1 - tile) * (1 - late)
-    end = place // (n - n // 4)
-    turn = (k + half * end) % (n - 1)
-    other = turn + (turn + n - place) // n
-    return other * late + (n - 1 - other) * (1 - late)
+    inner = 0
+    k = (k + half * inner) % (n - 1)
+    turn = k - half
+    near = turn + (turn + 2 * half - (tile - half * late)) // half - 1 + half * late
+    far = k + half * (1 - late)
+    is_near = k // half
+    return near * is_near + far * (1 - is_near)
 
 
 def exchange_kernel(n, nf, gs, wave, v_hbm, u_hbm, ranks_hbm, order_hbm,
@@ -33,8 +35,13 @@
     width = v_buf.shape[2] // 2
     chunk = sources // nf
     ng = nf // gs
-    rows = gs * chunk
+    pieces = [(p * gs, gs) for p in range(ng - 1)] + [(q, 1) for q in range(nf - gs, nf)]
     targets = [target(tile, k, n) for k in range(n - 1)]
+    half = n // 2
+    far, near = list(range(half)), list(range(half, n - 1))
+    F = lambda p: [(p, k) for k in far]
+    N = lambda p: [(p, k) for k in near]
+    plan = F(0)+N(0)+N(1)+N(2)+[(1,0),(2,0),(1,1),(2,1),(1,2),(1,3),(2,2),(2,3)]
 
     loads = [
         pltpu.make_async_copy(wave.at[0], x_buf, load_sems.at[0]),
@@ -54,13 +61,15 @@
             barrier, inc=1, device_id={"freq": (freq + hop) % nf}, device_id_type=MESH
         )
 
-    def group_of(p):
-        return (freq // gs + 1 + p) % ng
+    def receiver_of(q):
+        group = (freq // gs + 1 + q // gs) % ng
+        return group * gs + (q % gs if q < nf - gs else (freq + 1 + q) % gs)
 
     def send(p, k):
+        q, count = pieces[p]
         return pltpu.make_async_remote_copy(
-            src_ref=sending.at[k, group_of(p)],
-            dst_ref=landing.at[p, tile],
+            src_ref=sending.at[k, pl.ds(receiver_of(q), count)],
+            dst_ref=landing.at[tile, pl.ds(q, count)],
             send_sem=send_sems.at[p, k],
             recv_sem=recv_sems.at[p, tile],
             device_id={"tile": targets[k]},
@@ -68,18 +77,15 @@
         )
 
     def arrival(p, k):
+        q, count = pieces[p]
         return pltpu.make_async_remote_copy(
-            src_ref=sending.at[k, group_of(p)],
-            dst_ref=landing.at[p, targets[k]],
+            src_ref=sending.at[k, pl.ds(receiver_of(q), count)],
+            dst_ref=landing.at[targets[k], pl.ds(q, count)],
             send_sem=send_sems.at[p, k],
             recv_sem=recv_sems.at[p, targets[k]],
             device_id={"tile": targets[k]},
             device_id_type=MESH,
         )
-
-    def receiver_of(q):
-        p, c = q // gs, q % gs
-        return group_of(p) * gs + (freq + 1 + c) % gs
 
     def spec_send(q):
         return pltpu.make_async_remote_copy(
@@ -119,25 +125,30 @@
         imag = product[sources:, :width] - product[:sources, width:]
         real = jnp.where(keep, real, 0.0).astype(jnp.bfloat16)
         imag = jnp.where(keep, imag, 0.0).astype(jnp.bfloat16)
-        for g in range(ng):
-            sending[k, g, 0] = real[g * rows:(g + 1) * rows]
-            sending[k, g, 1] = imag[g * rows:(g + 1) * rows]
-
-    pairs = [list(range(k, min(k + 2, n - 1))) for k in range(0, n - 1, 2)]
-    for index, pair in enumerate(pairs):
-        for k in pair:
+        for c in range(nf):
+            sending[k, c, 0] = real[c * chunk:(c + 1) * chunk]
+            sending[k, c, 1] = imag[c * chunk:(c + 1) * chunk]
+
+    made = set()
+
+    def make(k):
+        if k not in made:
+            made.add(k)
             make_block(k, targets[k])
+
+    for index, (p, k) in enumerate(plan):
+        make(k)
         if index == 0:
             pl.semaphore_wait(barrier, n - 1 + nf - 1)
-        for p in range(ng):
-            for k in pair:
-                send(p, k).start()
+        elif index + 1 < len(plan):
+            make(plan[index + 1][1])
+        send(p, k).start()
     make_block(n - 1, tile)
 
     u_load.wait()
 
-    def apply_rows(pair, source):
-        real, imag = pair[0], pair[1]
+    def apply_rows(piece, source):
+        real, imag = (piece[:, c].reshape(-1, width) for c in range(2))
         left = jnp.concatenate(
             [jnp.concatenate([real, -imag], axis=1), jnp.concatenate([imag, real], axis=1)], axis=0
         )
@@ -145,32 +156,30 @@
             left, u_buf[source], (((1,), (1,)), ((), ())), preferred_element_type=jnp.float32
         )
 
-    half = n // 2
-    arrivals = list(range(half, n - 1)) + list(range(half))
-    for p in range(ng):
-        total = apply_rows(sending[n - 1, group_of(p)], tile)
+    arrivals = near + far
+    for p, (first, count) in enumerate(pieces):
+        total = apply_rows(sending[n - 1, pl.ds(receiver_of(first), count)], tile)
         for k in arrivals:
             arrival(p, k).wait_recv()
-            total = total + apply_rows(landing[p, targets[k]], targets[k])
-        spectrum = total.astype(jnp.bfloat16).reshape(2, gs, chunk, tile_rows)
-        for c in range(gs):
-            q = p * gs + c
-            place = (freq + 1 + c) % gs
-            part = spectrum[:, 0]
-            for other in range(1, gs):
-                part = jnp.where(place == other, spectrum[:, other], part)
-            if q < nf - 1:
-                spec_sending[q] = part
-                spec_send(q).start()
+            total = total + apply_rows(landing[targets[k], pl.ds(first, count)], targets[k])
+        spectrum = total.astype(jnp.bfloat16).reshape(2, count, chunk, tile_rows)
+        for c in range(count):
+            if first + c < nf - 1:
+                spec_sending[first + c] = spectrum[:, c]
+                spec_send(first + c).start()
             else:
-                spec_out[freq] = part
+                spec_out[freq] = spectrum[:, c]
 
     for q in range(nf - 1):
-        p, c = q // gs, q % gs
-        source = ((freq // gs + ng - 1 - p) % ng) * gs + (freq + 1 + c) % gs
-        spec_arrival(q, source).wait_recv()
-        spec_out[source] = spec_landing[source]
-    for p in range(ng):
+        group = (freq // gs + ng - 1 - q // gs) % ng
+        if q < nf - gs:
+            sources_of = [group * gs + c for c in range(gs)] if q % gs == 0 else []
+        else:
+            sources_of = [group * gs + (freq + nf - 1 - q) % gs]
+        for source in sources_of:
+            spec_arrival(q, source).wait_recv()
+            spec_out[source] = spec_landing[source]
+    for p in range(len(pieces)):
         for k in range(n - 1):
             send(p, k).wait_send()
     for q in range(nf - 1):
@@ -251,14 +260,14 @@
             pltpu.VMEM((n, tile_rows, double_width), bf16),
             pltpu.SMEM(tile_ranks.shape, jnp.int32),
             pltpu.SMEM(row_order.shape, jnp.int32),
-            pltpu.VMEM((n, ng, 2, gs * chunk, width), bf16),
-            pltpu.VMEM((ng, n, 2, gs * chunk, width), bf16),
+            pltpu.VMEM((n, nf, 2, chunk, width), bf16),
+            pltpu.VMEM((n, nf, 2, chunk, width), bf16),
             pltpu.VMEM((nf - 1, 2, chunk, tile_rows), bf16),
             pltpu.VMEM((nf, 2, chunk, tile_rows), bf16),
             pltpu.SemaphoreType.DMA((4,)),
             pltpu.SemaphoreType.DMA((n,)),
-            pltpu.SemaphoreType.DMA((ng, n)),
-            pltpu.SemaphoreType.DMA((ng, n)),
+            pltpu.SemaphoreType.DMA((ng - 1 + gs, n)),
+            pltpu.SemaphoreType.DMA((ng - 1 + gs, n)),
             pltpu.SemaphoreType.DMA((nf,)),
             pltpu.SemaphoreType.DMA((nf,)),
         ],

time: 21.6 us -> 20 us (0.926)
  Pallas kernels: 21.5 us -> 19.8 us
    pallas_call x1, Pallas kernels: 20.5 us -> 18.9 us  [body(): pl.pallas_call(functools.partial(exchange_kernel, n, nf, gs), out_shape=j...]
where the time goes in v2:
time: 20 us; the launch traced here: 19.9 us
  Pallas kernels  19.8 us (99%)
    pallas_call x1, Pallas kernels, body(): pl.pallas_call(functools.partial(exchange_kernel, n, nf, gs), out_shape=j...  18.9 us
    pallas_call x1, Pallas kernels, body(): pl.pallas_call(functools.partial(shrink_kernel, nf, nt), out_shape=jax.Sh...  0.96 us

profile of v2, /device:TPU:0, one launch (start us, length us, event | category | flops | bytes accessed | tf_op | source)
XLA Modules:
  0.0 19.9 jit_solution(10178312476590621343)
XLA Ops:
  0.0 0.0 copy-start
  0.0 18.9 %exchange.1.spec = bf16[4,2,32,384]{3,2,1,0:T(8,128)(2,1)S(1)} custom-call(bf16[1,384,256]{2,1,0:T(8,128)(2,1)} %wave.1, bf16[1,1,8,384,256]{4,3,2,1,0:T(8,128)(2,1)} %v_hbm.1, bf16[1,1,8,384,256]{4,3,2,1,0:T(8,128)(2,1)} %u_hbm.1, s32[8,8]{1,0:T(8,128)} %ranks_hbm.1, s32[8]{0:T(128)} %order_hbm.1), custom_call_target="tpu_custom_call" | custom-call | tf_op jit(solution)/shard_map/exchange/pallas_call | solution.py:252
  18.9 0.0 copy-done
  18.9 1.0 %shrink.1 = f32[12,32,384]{2,1,0:T(8,128)} custom-call(bf16[4,2,32,384]{3,2,1,0:T(8,128)(2,1)S(1)} %exchange.1.spec, f32[1,32]{1,0:T(1,128)S(1)} %bitcast.1), custom_call_target="tpu_custom_call" | custom-call | tf_op jit(solution)/shard_map/shrink/pallas_call | solution.py:279
Async XLA Ops:
  0.0 18.9 %copy-start = (f32[32]{0:T(128)S(1)}, f32[32]{0:T(128)}, u32[]{:S(2)}) copy-start(f32[32]{0:T(128)} %param.11) | copy-start | bytes 388

commit v3 on v2

--- a/solution.py
+++ b/solution.py
@@ -14,13 +14,9 @@
 def target(tile, k, n):
     half = n // 2
     late = tile // half
-    inner = 0
-    k = (k + half * inner) % (n - 1)
-    turn = k - half
-    near = turn + (turn + 2 * half - (tile - half * late)) // half - 1 + half * late
-    far = k + half * (1 - late)
-    is_near = k // half
-    return near * is_near + far * (1 - is_near)
+    place = tile * late + (n - 1 - tile) * (1 - late)
+    other = k + (k + n - place) // n
+    return other * late + (n - 1 - other) * (1 - late)
 
 
 def exchange_kernel(n, nf, gs, wave, v_hbm, u_hbm, ranks_hbm, order_hbm,
@@ -39,9 +35,11 @@
     targets = [target(tile, k, n) for k in range(n - 1)]
     half = n // 2
     far, near = list(range(half)), list(range(half, n - 1))
-    F = lambda p: [(p, k) for k in far]
-    N = lambda p: [(p, k) for k in near]
-    plan = F(0)+N(0)+N(1)+N(2)+[(1,0),(2,0),(1,1),(2,1),(1,2),(1,3),(2,2),(2,3)]
+    later = range(1, len(pieces))
+    plan = [(0, k) for k in far[:half // 2]]
+    plan += [(p, k) for k in near for p in range(len(pieces))]
+    plan += [(0, k) for k in far[half // 2:]]
+    plan += [(p, k) for k in far for p in later]
 
     loads = [
         pltpu.make_async_copy(wave.at[0], x_buf, load_sems.at[0]),

time: 20 us -> 19.6 us (0.980)
  Pallas kernels: 19.8 us -> 19.4 us
    pallas_call x1, Pallas kernels: 18.9 us -> 18.5 us  [body(): pl.pallas_call(functools.partial(exchange_kernel, n, nf, gs), out_shape=j...]
where the time goes in v3:
time: 19.6 us; the launch traced here: 19.5 us
  Pallas kernels  19.4 us (99%)
    pallas_call x1, Pallas kernels, body(): pl.pallas_call(functools.partial(exchange_kernel, n, nf, gs), out_shape=j...  18.5 us
    pallas_call x1, Pallas kernels, body(): pl.pallas_call(functools.partial(shrink_kernel, nf, nt), out_shape=jax.Sh...  0.96 us

profile of v3, /device:TPU:0, one launch (start us, length us, event | category | flops | bytes accessed | tf_op | source)
XLA Modules:
  0.0 19.5 jit_solution(10156237892287034538)
XLA Ops:
  0.0 0.0 copy-start
  0.0 18.5 %exchange.1.spec = bf16[4,2,32,384]{3,2,1,0:T(8,128)(2,1)S(1)} custom-call(bf16[1,384,256]{2,1,0:T(8,128)(2,1)} %wave.1, bf16[1,1,8,384,256]{4,3,2,1,0:T(8,128)(2,1)} %v_hbm.1, bf16[1,1,8,384,256]{4,3,2,1,0:T(8,128)(2,1)} %u_hbm.1, s32[8,8]{1,0:T(8,128)} %ranks_hbm.1, s32[8]{0:T(128)} %order_hbm.1), custom_call_target="tpu_custom_call" | custom-call | tf_op jit(solution)/shard_map/exchange/pallas_call | solution.py:250
  18.5 0.0 copy-done
  18.5 1.0 %shrink.1 = f32[12,32,384]{2,1,0:T(8,128)} custom-call(bf16[4,2,32,384]{3,2,1,0:T(8,128)(2,1)S(1)} %exchange.1.spec, f32[1,32]{1,0:T(1,128)S(1)} %bitcast.1), custom_call_target="tpu_custom_call" | custom-call | tf_op jit(solution)/shard_map/shrink/pallas_call | solution.py:277
Async XLA Ops:
  0.0 18.5 %copy-start = (f32[32]{0:T(128)S(1)}, f32[32]{0:T(128)}, u32[]{:S(2)}) copy-start(f32[32]{0:T(128)} %param.11) | copy-start | bytes 388

commit v4 on v3

--- a/solution.py
+++ b/solution.py
@@ -154,7 +154,7 @@
             left, u_buf[source], (((1,), (1,)), ((), ())), preferred_element_type=jnp.float32
         )
 
-    arrivals = near + far
+    arrivals = near[::-1] + far
     for p, (first, count) in enumerate(pieces):
         total = apply_rows(sending[n - 1, pl.ds(receiver_of(first), count)], tile)
         for k in arrivals:

time: 19.6 us -> 19.6 us (level)
  no operation moved by 1% of the time
where the time goes in v4:
time: 19.6 us; the launch traced here: 19.5 us
  Pallas kernels  19.4 us (99%)
    pallas_call x1, Pallas kernels, body(): pl.pallas_call(functools.partial(exchange_kernel, n, nf, gs), out_shape=j...  18.5 us
    pallas_call x1, Pallas kernels, body(): pl.pallas_call(functools.partial(shrink_kernel, nf, nt), out_shape=jax.Sh...  0.96 us

profile of v4, /device:TPU:0, one launch (start us, length us, event | category | flops | bytes accessed | tf_op | source)
XLA Modules:
  0.0 19.5 jit_solution(15163628593124403890)
XLA Ops:
  0.0 0.0 copy-start
  0.0 18.5 %exchange.1.spec = bf16[4,2,32,384]{3,2,1,0:T(8,128)(2,1)S(1)} custom-call(bf16[1,384,256]{2,1,0:T(8,128)(2,1)} %wave.1, bf16[1,1,8,384,256]{4,3,2,1,0:T(8,128)(2,1)} %v_hbm.1, bf16[1,1,8,384,256]{4,3,2,1,0:T(8,128)(2,1)} %u_hbm.1, s32[8,8]{1,0:T(8,128)} %ranks_hbm.1, s32[8]{0:T(128)} %order_hbm.1), custom_call_target="tpu_custom_call" | custom-call | tf_op jit(solution)/shard_map/exchange/pallas_call | solution.py:250
  18.5 0.0 copy-done
  18.5 1.0 %shrink.1 = f32[12,32,384]{2,1,0:T(8,128)} custom-call(bf16[4,2,32,384]{3,2,1,0:T(8,128)(2,1)S(1)} %exchange.1.spec, f32[1,32]{1,0:T(1,128)S(1)} %bitcast.1), custom_call_target="tpu_custom_call" | custom-call | tf_op jit(solution)/shard_map/shrink/pallas_call | solution.py:277
Async XLA Ops:
  0.0 18.5 %copy-start = (f32[32]{0:T(128)S(1)}, f32[32]{0:T(128)}, u32[]{:S(2)}) copy-start(f32[32]{0:T(128)} %param.11) | copy-start | bytes 388

commit v5 on v3

--- a/solution.py
+++ b/solution.py
@@ -48,7 +48,7 @@
     ]
     v_loads = [pltpu.make_async_copy(v_hbm.at[0, 0, i], v_buf.at[i], v_sems.at[i]) for i in range(n)]
     u_load = pltpu.make_async_copy(u_hbm.at[0, 0], u_buf, load_sems.at[1])
-    for load in loads + v_loads:
+    for load in loads:
         load.start()
 
     barrier = pltpu.get_barrier_semaphore()
@@ -58,6 +58,9 @@
         pl.semaphore_signal(
             barrier, inc=1, device_id={"freq": (freq + hop) % nf}, device_id_type=MESH
         )
+
+    for load in v_loads:
+        load.start()
 
     def receiver_of(q):
         group = (freq // gs + 1 + q // gs) % ng

time: 19.6 us -> 19.5 us (level)
  no operation moved by 1% of the time
where the time goes in v5:
time: 19.5 us; the launch traced here: 19.4 us
  Pallas kernels  19.4 us (99%)
    pallas_call x1, Pallas kernels, body(): pl.pallas_call(functools.partial(exchange_kernel, n, nf, gs), out_shape=j...  18.4 us
    pallas_call x1, Pallas kernels, body(): pl.pallas_call(functools.partial(shrink_kernel, nf, nt), out_shape=jax.Sh...  0.96 us

profile of v5, /device:TPU:0, one launch (start us, length us, event | category | flops | bytes accessed | tf_op | source)
XLA Modules:
  0.0 19.4 jit_solution(5002940288168820501)
XLA Ops:
  0.0 0.0 copy-start
  0.0 18.4 %exchange.1.spec = bf16[4,2,32,384]{3,2,1,0:T(8,128)(2,1)S(1)} custom-call(bf16[1,384,256]{2,1,0:T(8,128)(2,1)} %wave.1, bf16[1,1,8,384,256]{4,3,2,1,0:T(8,128)(2,1)} %v_hbm.1, bf16[1,1,8,384,256]{4,3,2,1,0:T(8,128)(2,1)} %u_hbm.1, s32[8,8]{1,0:T(8,128)} %ranks_hbm.1, s32[8]{0:T(128)} %order_hbm.1), custom_call_target="tpu_custom_call" | custom-call | tf_op jit(solution)/shard_map/exchange/pallas_call | solution.py:253
  18.4 0.0 copy-done
  18.4 1.0 %shrink.1 = f32[12,32,384]{2,1,0:T(8,128)} custom-call(bf16[4,2,32,384]{3,2,1,0:T(8,128)(2,1)S(1)} %exchange.1.spec, f32[1,32]{1,0:T(1,128)S(1)} %bitcast.1), custom_call_target="tpu_custom_call" | custom-call | tf_op jit(solution)/shard_map/shrink/pallas_call | solution.py:280
Async XLA Ops:
  0.0 18.4 %copy-start = (f32[32]{0:T(128)S(1)}, f32[32]{0:T(128)}, u32[]{:S(2)}) copy-start(f32[32]{0:T(128)} %param.11) | copy-start | bytes 388
